TPU v7x, 512 devices: a whole 4x4x16 slice. The times are simulated.
512 devices in a mesh: expert: 128 (over z, y_hi, x), half: 4 (over y_lo, core).
Axes of the slice: x: 4, y: 4 (y_hi: 2, y_lo: 2; y = y_hi * 2 + y_lo), z: 16, core: 2. Of those that a mesh axis runs over, the one named last changes fastest.
Arguments:
- tokens: bfloat16 [131072, 1024], P(('expert', 'half')), may hold values from -6 to 6
- router: bfloat16 [1024, 256], replicated, may hold values from -1 to 1
- w_in: bfloat16 [128, 1024, 3072], P('expert', None, 'half'), may hold values from -0.1875 to 0.1875
- w_out: bfloat16 [128, 3072, 1024], P('expert', 'half'), may hold values from -0.109375 to 0.109375
Outputs:
- mixed: bfloat16 [131072, 1024], P(('expert', 'half'))
All inputs are finite; a program needn't handle non-finite values.
Results may differ from a plain program's by a relative error of at most 0.018.
Values may be sent and summed in bfloat16 or wider, within the bound.
No kernel may reach another device: no remote copies, remote signals or barrier semaphores. Data moves between devices by JAX's collectives and lax.ppermute only.
A program may use at most 64 MiB of HBM per device.

v0:
```python
import jax
import jax.numpy as jnp
from jax import lax
from jax.sharding import PartitionSpec as P

SLOTS = 2
PATCHES = 256


def from_everyone(value, axis):
    length = lax.axis_size(axis)
    return lax.all_to_all(
        jnp.broadcast_to(value[None], (length, *value.shape)), axis, 0, 0, tiled=True
    )


def in_order(parts, dim):
    parts = jnp.moveaxis(parts, 0, dim)
    dims = parts.shape
    return parts.reshape(*dims[:dim], dims[dim] * dims[dim + 1], *dims[dim + 2 :])


def gathered_copies(value, axis, dim):
    parts = from_everyone(value, axis)
    return in_order(parts, dim)


def cut_along(value, dim, length):
    before, after = (value.shape[:dim], value.shape[dim + 1 :])
    return jnp.moveaxis(value.reshape(*before, length, -1, *after), dim, 0)


def summed_on_arrival(value, axis, dim):
    parts = cut_along(value, dim, lax.axis_size(axis))
    arrived = lax.all_to_all(parts, axis, split_axis=0, concat_axis=0, tiled=True)
    return arrived.astype(jnp.float32).sum(axis=0)


def expert_quarter(rows, first, second):
    hidden = jax.nn.gelu(
        jnp.einsum("erd,edf->erf", rows, first, preferred_element_type=jnp.float32)
    ).astype(jnp.bfloat16)
    return jnp.einsum("erf,efd->erd", hidden, second, preferred_element_type=jnp.float32)


def on_device(tokens, router, w_in, w_out):
    width = tokens.shape[1]
    images = tokens.shape[0] // PATCHES
    experts_all = router.shape[1] // SLOTS
    picture = tokens.reshape(images, PATCHES, width)
    logits = jnp.einsum("imd,dc->imc", picture, router, preferred_element_type=jnp.float32)
    dispatch = jax.nn.softmax(logits, axis=1).astype(jnp.bfloat16)
    combine = jax.nn.softmax(logits, axis=2).astype(jnp.bfloat16)
    slot_input = jnp.einsum(
        "imc,imd->icd", dispatch, picture, preferred_element_type=jnp.float32
    ).astype(jnp.bfloat16)
    outgoing = slot_input.reshape(images, experts_all, SLOTS, width)
    arrived = lax.all_to_all(outgoing, "expert", split_axis=1, concat_axis=0, tiled=True)
    local_experts = arrived.shape[1]
    slot_rows_local = jnp.transpose(arrived, (1, 0, 2, 3)).reshape(local_experts, -1, width)
    terms = expert_quarter(gathered_copies(slot_rows_local, "half", 1), w_in, w_out)
    result = summed_on_arrival(terms.astype(jnp.bfloat16), "half", 1)
    back = jnp.transpose(
        result.astype(jnp.bfloat16).reshape(local_experts, -1, SLOTS, width), (1, 0, 2, 3)
    )
    returned = lax.all_to_all(back, "expert", split_axis=0, concat_axis=1, tiled=True)
    slot_output = returned.reshape(images, experts_all * SLOTS, width)
    mixed = jnp.einsum(
        "imc,icd->imd", combine, slot_output, preferred_element_type=jnp.float32
    ).astype(jnp.bfloat16)
    return mixed.reshape(-1, width)


def solution(mesh):
    return jax.shard_map(
        on_device,
        mesh=mesh,
        in_specs=(
            P(("expert", "half"), None),
            P(),
            P("expert", None, "half"),
            P("expert", "half", None),
        ),
        out_specs=P(("expert", "half"), None),
        check_vma=False,
    )
```

profile of v0, /device:TPU:32, one launch (start us, length us, event | category | flops | bytes accessed | tf_op | source)
XLA Modules:
  0.0 171.6 jit_solution(13309101023838386148)
XLA Ops:
  0.0 0.0 copy-start
  0.0 1.7 fusion.30
  1.7 0.2 fusion.20
  1.9 1.4 convolution_convert_fusion.2
  3.3 0.2 reshape.92
  3.5 56.3 %all_to_all.28 = bf16[1,128,2,1024]{3,2,0,1:T(2,128)(2,1)S(1)} all-to-all(bf16[1,128,2,1024]{3,2,0,1:T(2,128)(2,1)S(1)} %bitcast.24), channel_id=1, replica_groups=mesh['expert'=128,'half'=4] {'expert'}, dimensions={1} | all-to-all | bytes 1048576 | tf_op jit(solution)/shard_map/all_to_all | solution.py:58
  59.8 0.2 broadcast_in_dim.4
  60.0 0.3 broadcast_in_dim.5
  60.3 0.0 copy-start.1
  60.3 29.0 %all_to_all.29 = bf16[4,1,256,1024]{3,2,1,0:T(8,128)(2,1)} all-to-all(bf16[4,1,256,1024]{3,2,1,0:T(8,128)(2,1)S(1)} %broadcast_in_dim.5), channel_id=1, replica_groups=mesh['expert'=128,'half'=4] {'half'}, dimensions={0} | all-to-all | bytes 4194304 | tf_op jit(solution)/shard_map/all_to_all | solution.py:12
  89.3 0.0 copy-done
  89.3 0.0 copy-done.1
  89.3 7.4 %convolution_convert_fusion = bf16[1024,1024]{1,0:T(8,128)(2,1)} fusion(bf16[1,768,1024]{2,1,0:T(8,128)(2,1)S(1)} %copy-done, bf16[1024,1024]{1,0:T(8,128)(2,1)} %bitcast.22, bf16[1,1024,768]{2,1,0:T(8,128)(2,1)S(1)} %copy-done.1), kind=kOutput, calls=%fused_computation.9 | convolution fusion | flops 3229351936 | bytes 7340032 | tf_op jit(solution)/shard_map/erf,efd->erd/dot_general | solution.py:43
  96.8 30.1 %all_to_all.30 = bf16[4,1,256,1024]{3,2,1,0:T(8,128)(2,1)} all-to-all(bf16[4,1,256,1024]{3,2,1,0:T(8,128)(2,1)} %bitcast.23), channel_id=1, replica_groups=mesh['expert'=128,'half'=4] {'half'}, dimensions={0} | all-to-all | bytes 4194304 | tf_op jit(solution)/shard_map/all_to_all | solution.py:35
  126.9 2.0 %reduce_sum.32 = bf16[256,1024]{1,0:T(8,128)(2,1)S(1)} reduce(bf16[4,1,256,1024]{3,2,1,0:T(8,128)(2,1)} %all_to_all.30, bf16[]{:T(256)} %constant.14.clone.1), dimensions={0,1}, to_apply=%region_4.0 | reduce | flops 786432 | bytes 2621442 | tf_op jit(solution)/shard_map/reduce_sum | solution.py:36
  128.9 0.2 transpose_reshape.7
  129.1 41.1 %all_to_all.31 = bf16[128,1,2,1024]{3,2,1,0:T(2,128)(2,1)S(1)} all-to-all(bf16[128,1,2,1024]{3,2,1,0:T(2,128)(2,1)S(1)} %transpose_reshape.7), channel_id=1, replica_groups=mesh['expert'=128,'half'=4] {'expert'}, dimensions={0} | all-to-all | bytes 1048576 | tf_op jit(solution)/shard_map/all_to_all | solution.py:66
  170.3 0.2 reshape.96
  170.5 1.2 convolution_convert_fusion.1
Async XLA Ops:
  0.0 89.3 %copy-start = (bf16[1,768,1024]{2,1,0:T(8,128)(2,1)S(1)}, bf16[1,768,1024]{2,1,0:T(8,128)(2,1)}, u32[]{:S(2)}) copy-start(bf16[1,768,1024]{2,1,0:T(8,128)(2,1)} %param.7) | copy-start | bytes 4718596
  60.3 29.1 %copy-start.1 = (bf16[1,1024,768]{2,1,0:T(8,128)(2,1)S(1)}, bf16[1,1024,768]{2,1,0:T(8,128)(2,1)}, u32[]{:S(2)}) copy-start(bf16[1,1024,768]{2,1,0:T(8,128)(2,1)} %param.6) | copy-start | bytes 4718596
where the time goes:
time: 172 us
  blocking collectives  157 us (91%)
  matrix products  11.7 us (7%)
  other arithmetic  2.22 us (1%)
    all_to_all x1, blocking collectives, on_device(): lax.all_to_all(outgoing, 'expert', split_axis=1, concat_axis=0, tiled=True)  56.3 us
    all_to_all x1, blocking collectives, on_device(): lax.all_to_all(back, 'expert', split_axis=0, concat_axis=1, tiled=True)  41.1 us
    all_to_all x1, blocking collectives, summed_on_arrival(): lax.all_to_all(parts, axis, split_axis=0, concat_axis=0, tiled=True)  30.1 us
    all_to_all x1, blocking collectives, from_everyone(): lax.all_to_all(jnp.broadcast_to(value[None], (length, *value.shape)), axi...  29 us
    dot_general x1, matrix products, expert_quarter(): jnp.einsum('erf,efd->erd', hidden, second, preferred_element_type=jnp.flo...  7.43 us

commit v1 on v0

v1 whole, which is shorter than its diff:
```python
import jax
import jax.numpy as jnp
from jax import lax
from jax.sharding import PartitionSpec as P

SLOTS = 2
PIECES = 2


OTHER_CORE = [(0, 1), (1, 0), (2, 3), (3, 2)]
OTHER_CHIP = [(0, 2), (1, 3), (2, 0), (3, 1)]


def experts_half(rows, first, second):
    hidden = jax.nn.gelu(
        jnp.einsum("rd,df->rf", rows, first, preferred_element_type=jnp.float32)
    ).astype(jnp.bfloat16)
    return jnp.einsum("rf,fd->rd", hidden, second, preferred_element_type=jnp.float32)


def on_device(tokens, router, w_in, w_out):
    width = tokens.shape[1]
    experts_all = router.shape[1] // SLOTS
    logits = jnp.einsum("md,dc->mc", tokens, router, preferred_element_type=jnp.float32)
    dispatch = jax.nn.softmax(logits, axis=0).astype(jnp.bfloat16)
    combine = jax.nn.softmax(logits, axis=1).astype(jnp.bfloat16)
    slot_input = jnp.einsum(
        "mc,md->cd", dispatch, tokens, preferred_element_type=jnp.float32
    ).astype(jnp.bfloat16)
    arrived = lax.all_to_all(
        slot_input.reshape(experts_all, SLOTS, width), "expert", 0, 0, tiled=True
    )
    rows = arrived.reshape(-1, width)
    first = jnp.concatenate([w_in[0], lax.ppermute(w_in[0], "half", OTHER_CORE)], axis=1)
    second = jnp.concatenate([w_out[0], lax.ppermute(w_out[0], "half", OTHER_CORE)], axis=0)
    pieces = jnp.split(rows, PIECES)
    others = [lax.ppermute(piece, "half", OTHER_CHIP) for piece in pieces]
    own = experts_half(rows, first, second)
    own, others[0] = lax.optimization_barrier((own, others[0]))
    terms = [experts_half(piece, first, second).astype(jnp.bfloat16) for piece in others]
    returned = [lax.ppermute(term, "half", OTHER_CHIP) for term in terms]
    result = (own + jnp.concatenate(returned).astype(jnp.float32)).astype(jnp.bfloat16)
    slot_output = lax.all_to_all(
        result.reshape(experts_all, SLOTS, width), "expert", 0, 0, tiled=True
    ).reshape(-1, width)
    return jnp.einsum(
        "mc,cd->md", combine, slot_output, preferred_element_type=jnp.float32
    ).astype(jnp.bfloat16)


def solution(mesh):
    return jax.shard_map(
        on_device,
        mesh=mesh,
        in_specs=(
            P(("expert", "half"), None),
            P(),
            P("expert", None, "half"),
            P("expert", "half", None),
        ),
        out_specs=P(("expert", "half"), None),
        check_vma=False,
    )
```

time: 172 us -> 138 us (0.80)
  blocking collectives: 157 us -> 41.2 us
  waiting for transfers between devices: 0 us -> 38.5 us
  starting transfers between devices: 0 us -> 37.7 us
  matrix products: 11.7 us -> 16 us
  local copies, waits for them, and re-layouts: 1.08 us -> 3.19 us
  other arithmetic: 2.22 us -> 0.34 us
    all_to_all x4 -> x1, blocking collectives: 157 us -> 41.2 us  [on_device(): lax.all_to_all(result.reshape(experts_all, SLOTS, width), 'expert', 0, 0,...]
    all_to_all x0 -> x1, waiting for transfers between devices: none -> 30.5 us  [on_device(): lax.all_to_all(slot_input.reshape(experts_all, SLOTS, width), 'expert', 0...]
    all_to_all x0 -> x1, starting transfers between devices: none -> 21.6 us  [on_device(): lax.all_to_all(slot_input.reshape(experts_all, SLOTS, width), 'expert', 0...]
    ppermute x0 -> x6, starting transfers between devices: none -> 16 us  [the longest x2 5.84 us: on_device(): others = [lax.ppermute(piece, 'half', OTHER_CHIP) for piece in pieces]]
    ppermute x0 -> x6, waiting for transfers between devices: none -> 8.01 us  [the longest x2 5.17 us: on_device(): returned = [lax.ppermute(term, 'half', OTHER_CHIP) for term in terms]]
    dot_general x4 -> x6, matrix products: 11.7 us -> 16 us  [the longest x3 13.1 us: experts_half(): jnp.einsum('rf,fd->rd', hidden, second, preferred_element_type=jnp.float32)]
    reduce_sum x2 -> x1, other arithmetic: 2.22 us -> 0.2 us  [on_device(): combine = jax.nn.softmax(logits, axis=1).astype(jnp.bfloat16)]
  transfers between devices with their start and end apart: 0 -> 7, of which waited for: 0 -> 3; matrix products, arithmetic and copies ran while one was open for 0% -> 10% of each run, Pallas kernels for 0% -> 0%
where the time goes in v1:
time: 138 us; the launch traced here: 137 us
  blocking collectives  41.2 us (30%)
  waiting for transfers between devices  38.5 us (28%)
  starting transfers between devices  37.7 us (27%)
  matrix products  16 us (12%)
  local copies, waits for them, and re-layouts  3.19 us (2%)
    all_to_all x1, blocking collectives, on_device(): lax.all_to_all(result.reshape(experts_all, SLOTS, width), 'expert', 0, 0,...  41.2 us
    all_to_all x1, waiting for transfers between devices, on_device(): lax.all_to_all(slot_input.reshape(experts_all, SLOTS, width), 'expert', 0...  30.5 us
    all_to_all x1, starting transfers between devices, on_device(): lax.all_to_all(slot_input.reshape(experts_all, SLOTS, width), 'expert', 0...  21.6 us
    dot_general x3, matrix products, experts_half(): jnp.einsum('rf,fd->rd', hidden, second, preferred_element_type=jnp.float32)  13.1 us
    ppermute x2, starting transfers between devices, on_device(): others = [lax.ppermute(piece, 'half', OTHER_CHIP) for piece in pieces]  5.84 us
    ppermute x2, starting transfers between devices, on_device(): returned = [lax.ppermute(term, 'half', OTHER_CHIP) for term in terms]  5.84 us
    ppermute x2, waiting for transfers between devices, on_device(): returned = [lax.ppermute(term, 'half', OTHER_CHIP) for term in terms]  5.17 us
    ppermute x2, waiting for transfers between devices, on_device(): others = [lax.ppermute(piece, 'half', OTHER_CHIP) for piece in pieces]  2.83 us
  transfers between devices with their start and end apart: 7, of which 3 were waited for; matrix products, arithmetic and copies ran while one was open for 10% of the time, Pallas kernels for 0%

profile of v1, /device:TPU:32, one launch (start us, length us, event | category | flops | bytes accessed | tf_op | source)
XLA Modules:
  0.0 137.2 jit_solution(3031588851155856208)
XLA Ops:
  0.0 0.0 copy-start
  0.0 1.0 copy-done
  1.0 1.4 %fusion.60 = (f32[256]{0:T(256)S(1)}, f32[256]{0:T(256)S(1)}, f32[256,256]{1,0:T(8,128)S(1)}) fusion(bf16[256,1024]{1,0:T(8,128)(2,1)S(1)} %copy-done, bf16[1024,256]{1,0:T(8,128)(2,1)} %param.5), kind=kOutput, calls=%fused_computation.71 | convolution fusion | flops 134348288 | bytes 1312768 | tf_op jit(solution)/shard_map/md,dc->mc/dot_general | solution.py:24
  2.5 0.2 fusion.36
  2.7 0.3 convolution_convert_fusion.1
  3.0 1.0 reshape.18
  4.0 21.6 %all-to-all-start = ((bf16[128,2,1024]{2,1,0:T(2,128)(2,1)}), bf16[128,2,1024]{2,1,0:T(2,128)(2,1)S(1)}, u32[]{:S(2)}, u32[]{:S(2)}) async-start(bf16[128,2,1024]{2,1,0:T(2,128)(2,1)} %reshape.18), calls=%async_computation | async-start | bytes 1048576 | tf_op jit(solution)/shard_map/all_to_all | solution.py:30
  25.6 1.9 %collective-permute-start = (bf16[1024,768]{1,0:T(8,128)(2,1)}, bf16[1024,768]{1,0:T(8,128)(2,1)}, u32[]{:S(2)}, u32[]{:S(2)}) collective-permute-start(bf16[1024,768]{1,0:T(8,128)(2,1)} %bitcast), channel_id=1, source_target_pairs={{0,1},{1,0},{2,3},{3,2},{4,5},{5,4},{6,7},{7,6},{8,9},{9,8},{10,11... | collective-permute-start | bytes 4718600 | tf_op jit(solution)/shard_map/ppermute | solution.py:34
  27.6 2.4 %collective-permute-start.1 = (bf16[768,1024]{1,0:T(8,128)(2,1)}, bf16[768,1024]{1,0:T(8,128)(2,1)}, u32[]{:S(2)}, u32[]{:S(2)}) collective-permute-start(bf16[768,1024]{1,0:T(8,128)(2,1)} %bitcast.1), channel_id=1, source_target_pairs={{0,1},{1,0},{2,3},{3,2},{4,5},{5,4},{6,7},{7,6},{8,9},{9,8},{10,11... | collective-permute-start | bytes 4718600 | tf_op jit(solution)/shard_map/ppermute | solution.py:35
  30.0 30.5 %all-to-all-done = bf16[128,2,1024]{2,1,0:T(2,128)(2,1)S(1)} async-done(((bf16[128,2,1024]{2,1,0:T(2,128)(2,1)}), bf16[128,2,1024]{2,1,0:T(2,128)(2,1)S(1)}, u32[]{:S(2)}, u32[]{:S(2)}) %all-to-all-start) | async-done | bytes 524320 | tf_op jit(solution)/shard_map/all_to_all | solution.py:30
  60.5 0.4 fusion.61
  60.9 0.1 split.13
  61.0 0.1 split.11
  61.1 2.6 %collective-permute-start.2 = (bf16[128,1024]{1,0:T(8,128)(2,1)S(1)}, bf16[128,1024]{1,0:T(8,128)(2,1)}, u32[]{:S(2)}, u32[]{:S(2)}) collective-permute-start(bf16[128,1024]{1,0:T(8,128)(2,1)S(1)} %split.11), channel_id=1, source_target_pairs={{0,2},{1,3},{2,0},{3,1},{4,6},{5,7},{6,4},{7,5},{8,10},{9,11},{10,... | collective-permute-start | bytes 786440 | tf_op jit(solution)/shard_map/ppermute | solution.py:37
  63.7 3.3 %collective-permute-start.4 = (bf16[128,1024]{1,0:T(8,128)(2,1)S(1)}, bf16[128,1024]{1,0:T(8,128)(2,1)}, u32[]{:S(2)}, u32[]{:S(2)}) collective-permute-start(bf16[128,1024]{1,0:T(8,128)(2,1)S(1)} %split.13), channel_id=1, source_target_pairs={{0,2},{1,3},{2,0},{3,1},{4,6},{5,7},{6,4},{7,5},{8,10},{9,11},{10,... | collective-permute-start | bytes 786440 | tf_op jit(solution)/shard_map/ppermute | solution.py:37
  66.9 0.2 reshape.19
  67.1 0.0 collective-permute-done
  67.2 0.0 collective-permute-done.1
  67.2 4.8 %fusion.8 = f32[256,1024]{1,0:T(8,128)S(1)} fusion(bf16[768,1024]{1,0:T(8,128)(2,1)} %collective-permute-done.1, bf16[768,1024]{1,0:T(8,128)(2,1)} %bitcast.1, bf16[256,1024]{1,0:T(8,128)(2,1)S(1)} %reshape.19, bf16[1024,768]{1,0:T(8,128)(2,1)} %collective-permute-done, bf16[1024,768]{1,0:T(8,128)(2,1)} %bitcast), kind=kOutput, calls=%fused_computation.18 | convolution fusion | flops 1626734592 | bytes 7864320 | tf_op jit(solution)/shard_map/rf,fd->rd/dot_general | solution.py:18
  72.0 2.8 %collective-permute-done.4 = bf16[128,1024]{1,0:T(8,128)(2,1)} collective-permute-done((bf16[128,1024]{1,0:T(8,128)(2,1)S(1)}, bf16[128,1024]{1,0:T(8,128)(2,1)}, u32[]{:S(2)}, u32[]{:S(2)}) %collective-permute-start.4) | collective-permute-done | bytes 262176 | tf_op jit(solution)/shard_map/ppermute | solution.py:37
  74.8 4.2 %convolution_convert_fusion.2 = bf16[128,1024]{1,0:T(8,128)(2,1)S(1)} fusion(bf16[768,1024]{1,0:T(8,128)(2,1)} %collective-permute-done.1, bf16[768,1024]{1,0:T(8,128)(2,1)} %bitcast.1, bf16[128,1024]{1,0:T(8,128)(2,1)} %collective-permute-done.4, bf16[1024,768]{1,0:T(8,128)(2,1)} %collective-permute-done, bf16[1024,768]{1,0:T(8,128)(2,1)} %bitcast), kind=kOutput, calls=%fused_computation.13 | convolution fusion | flops 819789824 | bytes 6815744 | tf_op jit(solution)/shard_map/rf,fd->rd/dot_general | solution.py:18
  79.0 2.8 %collective-permute-start.5 = (bf16[128,1024]{1,0:T(8,128)(2,1)S(1)}, bf16[128,1024]{1,0:T(8,128)(2,1)S(1)}, u32[]{:S(2)}, u32[]{:S(2)}) collective-permute-start(bf16[128,1024]{1,0:T(8,128)(2,1)S(1)} %convolution_convert_fusion.2), channel_id=1, source_target_pairs={{0,2},{1,3},{2,0},{3,1},{4,6},{5,7},{6,4},{7,5},{8,10},{9,11},{10,... | collective-permute-start | bytes 786440 | tf_op jit(solution)/shard_map/ppermute | solution.py:41
  81.7 0.0 collective-permute-done.2
  81.8 4.2 %convolution_convert_fusion.3 = bf16[128,1024]{1,0:T(8,128)(2,1)S(1)} fusion(bf16[768,1024]{1,0:T(8,128)(2,1)} %collective-permute-done.1, bf16[768,1024]{1,0:T(8,128)(2,1)} %bitcast.1, bf16[128,1024]{1,0:T(8,128)(2,1)} %collective-permute-done.2, bf16[1024,768]{1,0:T(8,128)(2,1)} %collective-permute-done, bf16[1024,768]{1,0:T(8,128)(2,1)} %bitcast), kind=kOutput, calls=%fused_computation.14 | convolution fusion | flops 819789824 | bytes 6815744 | tf_op jit(solution)/shard_map/rf,fd->rd/dot_general | solution.py:18
  85.9 3.1 %collective-permute-start.3 = (bf16[128,1024]{1,0:T(8,128)(2,1)S(1)}, bf16[128,1024]{1,0:T(8,128)(2,1)S(1)}, u32[]{:S(2)}, u32[]{:S(2)}) collective-permute-start(bf16[128,1024]{1,0:T(8,128)(2,1)S(1)} %convolution_convert_fusion.3), channel_id=1, source_target_pairs={{0,2},{1,3},{2,0},{3,1},{4,6},{5,7},{6,4},{7,5},{8,10},{9,11},{10,... | collective-permute-start | bytes 786440 | tf_op jit(solution)/shard_map/ppermute | solution.py:41
  89.0 0.0 collective-permute-done.5
  89.0 5.2 %collective-permute-done.3 = bf16[128,1024]{1,0:T(8,128)(2,1)S(1)} collective-permute-done((bf16[128,1024]{1,0:T(8,128)(2,1)S(1)}, bf16[128,1024]{1,0:T(8,128)(2,1)S(1)}, u32[]{:S(2)}, u32[]{:S(2)}) %collective-permute-start.3) | collective-permute-done | bytes 262176 | tf_op jit(solution)/shard_map/ppermute | solution.py:41
  94.2 0.1 add_convert_fusion
  94.3 0.2 reshape.20
  94.6 41.2 %all_to_all.10 = bf16[128,2,1024]{2,1,0:T(2,128)(2,1)S(1)} all-to-all(bf16[128,2,1024]{2,1,0:T(2,128)(2,1)S(1)} %reshape.20), channel_id=1, replica_groups=mesh['expert'=128,'half'=4] {'expert'}, dimensions={0} | all-to-all | bytes 1048576 | tf_op jit(solution)/shard_map/all_to_all | solution.py:43
  135.8 0.2 reshape.21
  136.0 1.2 convolution_convert_fusion
Async XLA Ops:
  0.0 1.0 copy-start
  4.0 56.5 %all-to-all-start = ((bf16[128,2,1024]{2,1,0:T(2,128)(2,1)}), bf16[128,2,1024]{2,1,0:T(2,128)(2,1)S(1)}, u32[]{:S(2)}, u32[]{:S(2)}) async-start(bf16[128,2,1024]{2,1,0:T(2,128)(2,1)} %reshape.18), calls=%async_computation | async-start | bytes 1048576 | tf_op jit(solution)/shard_map/all_to_all | solution.py:30
  25.6 41.5 %collective-permute-start = (bf16[1024,768]{1,0:T(8,128)(2,1)}, bf16[1024,768]{1,0:T(8,128)(2,1)}, u32[]{:S(2)}, u32[]{:S(2)}) collective-permute-start(bf16[1024,768]{1,0:T(8,128)(2,1)} %bitcast), channel_id=1, source_target_pairs={{0,1},{1,0},{2,3},{3,2},{4,5},{5,4},{6,7},{7,6},{8,9},{9,8},{10,11... | collective-permute-start | bytes 4718600 | tf_op jit(solution)/shard_map/ppermute | solution.py:34
  27.6 39.6 %collective-permute-start.1 = (bf16[768,1024]{1,0:T(8,128)(2,1)}, bf16[768,1024]{1,0:T(8,128)(2,1)}, u32[]{:S(2)}, u32[]{:S(2)}) collective-permute-start(bf16[768,1024]{1,0:T(8,128)(2,1)} %bitcast.1), channel_id=1, source_target_pairs={{0,1},{1,0},{2,3},{3,2},{4,5},{5,4},{6,7},{7,6},{8,9},{9,8},{10,11... | collective-permute-start | bytes 4718600 | tf_op jit(solution)/shard_map/ppermute | solution.py:35
  61.1 20.7 %collective-permute-start.2 = (bf16[128,1024]{1,0:T(8,128)(2,1)S(1)}, bf16[128,1024]{1,0:T(8,128)(2,1)}, u32[]{:S(2)}, u32[]{:S(2)}) collective-permute-start(bf16[128,1024]{1,0:T(8,128)(2,1)S(1)} %split.11), channel_id=1, source_target_pairs={{0,2},{1,3},{2,0},{3,1},{4,6},{5,7},{6,4},{7,5},{8,10},{9,11},{10,... | collective-permute-start | bytes 786440 | tf_op jit(solution)/shard_map/ppermute | solution.py:37
  63.7 11.1 %collective-permute-start.4 = (bf16[128,1024]{1,0:T(8,128)(2,1)S(1)}, bf16[128,1024]{1,0:T(8,128)(2,1)}, u32[]{:S(2)}, u32[]{:S(2)}) collective-permute-start(bf16[128,1024]{1,0:T(8,128)(2,1)S(1)} %split.13), channel_id=1, source_target_pairs={{0,2},{1,3},{2,0},{3,1},{4,6},{5,7},{6,4},{7,5},{8,10},{9,11},{10,... | collective-permute-start | bytes 786440 | tf_op jit(solution)/shard_map/ppermute | solution.py:37
  79.0 10.0 %collective-permute-start.5 = (bf16[128,1024]{1,0:T(8,128)(2,1)S(1)}, bf16[128,1024]{1,0:T(8,128)(2,1)S(1)}, u32[]{:S(2)}, u32[]{:S(2)}) collective-permute-start(bf16[128,1024]{1,0:T(8,128)(2,1)S(1)} %convolution_convert_fusion.2), channel_id=1, source_target_pairs={{0,2},{1,3},{2,0},{3,1},{4,6},{5,7},{6,4},{7,5},{8,10},{9,11},{10,... | collective-permute-start | bytes 786440 | tf_op jit(solution)/shard_map/ppermute | solution.py:41
  85.9 8.3 %collective-permute-start.3 = (bf16[128,1024]{1,0:T(8,128)(2,1)S(1)}, bf16[128,1024]{1,0:T(8,128)(2,1)S(1)}, u32[]{:S(2)}, u32[]{:S(2)}) collective-permute-start(bf16[128,1024]{1,0:T(8,128)(2,1)S(1)} %convolution_convert_fusion.3), channel_id=1, source_target_pairs={{0,2},{1,3},{2,0},{3,1},{4,6},{5,7},{6,4},{7,5},{8,10},{9,11},{10,... | collective-permute-start | bytes 786440 | tf_op jit(solution)/shard_map/ppermute | solution.py:41

commit v2 on v1

--- a/solution.py
+++ b/solution.py
@@ -1,7 +1,10 @@
 import jax
 import jax.numpy as jnp
 from jax import lax
+from jax.experimental import pallas as pl
+from jax.experimental.pallas import tpu as pltpu
 from jax.sharding import PartitionSpec as P
+
 
 SLOTS = 2
 PIECES = 2
@@ -11,11 +14,65 @@
 OTHER_CHIP = [(0, 2), (1, 3), (2, 0), (3, 1)]
 
 
-def experts_half(rows, first, second):
-    hidden = jax.nn.gelu(
-        jnp.einsum("rd,df->rf", rows, first, preferred_element_type=jnp.float32)
-    ).astype(jnp.bfloat16)
-    return jnp.einsum("rf,fd->rd", hidden, second, preferred_element_type=jnp.float32)
+def mlp_kernel(rows_ref, in_ref, out_ref, terms_ref):
+    rows = rows_ref[...]
+    hidden = jax.nn.gelu(jnp.dot(rows, in_ref[...], preferred_element_type=jnp.float32))
+    terms_ref[...] = jnp.dot(
+        hidden.astype(jnp.bfloat16), out_ref[...], preferred_element_type=jnp.float32
+    ).astype(terms_ref.dtype)
+
+
+def loader_kernel(in_a, in_b, out_a, out_b, in_ref, out_ref, sems):
+    units = in_a.shape[1]
+    copies = [
+        pltpu.make_async_copy(source, target, sems.at[k])
+        for k, (source, target) in enumerate(
+            (
+                (in_a, in_ref.at[:, pl.ds(0, units)]),
+                (in_b, in_ref.at[:, pl.ds(units, units)]),
+                (out_a, out_ref.at[pl.ds(0, units)]),
+                (out_b, out_ref.at[pl.ds(units, units)]),
+            )
+        )
+    ]
+    for copy in copies:
+        copy.start()
+    for copy in copies:
+        copy.wait()
+
+
+def side_by_side(in_a, in_b, out_a, out_b):
+    width, units = in_a.shape
+    size = 4 * width * 2 * units
+    return pl.pallas_call(
+        loader_kernel,
+        out_shape=[
+            pltpu.VMEM((width, 2 * units), jnp.bfloat16),
+            pltpu.VMEM((2 * units, width), jnp.bfloat16),
+        ],
+        in_specs=[pl.BlockSpec(memory_space=pltpu.HBM)] * 4,
+        out_specs=[pl.BlockSpec(memory_space=pltpu.VMEM)] * 2,
+        scratch_shapes=[pltpu.SemaphoreType.DMA((4,))],
+        compiler_params=pltpu.CompilerParams(vmem_limit_bytes=16 << 20),
+        cost_estimate=pl.CostEstimate(flops=0, bytes_accessed=2 * size, transcendentals=0),
+    )(in_a, in_b, out_a, out_b)
+
+
+def experts_half(rows, weights, kind):
+    count, width = rows.shape
+    units = weights[0].shape[1]
+    return pl.pallas_call(
+        mlp_kernel,
+        out_shape=jax.ShapeDtypeStruct((count, width), kind),
+        in_specs=[pl.BlockSpec(memory_space=pltpu.VMEM)] * 3,
+        out_specs=pl.BlockSpec(memory_space=pltpu.VMEM),
+        compiler_params=pltpu.CompilerParams(vmem_limit_bytes=24 << 20),
+        cost_estimate=pl.CostEstimate(
+            flops=4 * count * width * units,
+            bytes_accessed=4 * width * units,
+            transcendentals=count * units,
+        ),
+    )(rows, *weights)
 
 
 def on_device(tokens, router, w_in, w_out):
@@ -30,14 +87,16 @@
     arrived = lax.all_to_all(
         slot_input.reshape(experts_all, SLOTS, width), "expert", 0, 0, tiled=True
     )
-    rows = arrived.reshape(-1, width)
-    first = jnp.concatenate([w_in[0], lax.ppermute(w_in[0], "half", OTHER_CORE)], axis=1)
-    second = jnp.concatenate([w_out[0], lax.ppermute(w_out[0], "half", OTHER_CORE)], axis=0)
-    pieces = jnp.split(rows, PIECES)
-    others = [lax.ppermute(piece, "half", OTHER_CHIP) for piece in pieces]
-    own = experts_half(rows, first, second)
-    own, others[0] = lax.optimization_barrier((own, others[0]))
-    terms = [experts_half(piece, first, second).astype(jnp.bfloat16) for piece in others]
+    rows = lax.optimization_barrier(arrived.reshape(-1, width))
+    in_b = lax.ppermute(w_in[0], "half", OTHER_CORE)
+    out_b = lax.ppermute(w_out[0], "half", OTHER_CORE)
+    weights = side_by_side(w_in[0], in_b, w_out[0], out_b)
+    others = []
+    for piece in jnp.split(rows, PIECES):
+        others.append(lax.ppermute(piece, "half", OTHER_CHIP))
+    terms = [experts_half(piece, weights, jnp.bfloat16) for piece in others]
+    rows, terms[0] = lax.optimization_barrier((rows, terms[0]))
+    own = experts_half(rows, weights, jnp.float32)
     returned = [lax.ppermute(term, "half", OTHER_CHIP) for term in terms]
     result = (own + jnp.concatenate(returned).astype(jnp.float32)).astype(jnp.bfloat16)
     slot_output = lax.all_to_all(

time: 138 us -> 129 us (0.935)
  matrix products: 16 us -> 2.91 us
  Pallas kernels: 0 us -> 6.17 us
  waiting for transfers between devices: 38.5 us -> 36.1 us
    dot_general x3 -> x0, matrix products: 13.1 us -> none  [experts_half(): jnp.einsum('rf,fd->rd', hidden, second, preferred_element_type=jnp.float32)]
    pallas_call x0 -> x4, Pallas kernels: none -> 6.17 us  [the longest x3 4.11 us: experts_half(): pl.pallas_call(mlp_kernel, out_shape=jax.ShapeDtypeStruct((count, width),...]
    unnamed x2 -> x6, local copies, waits for them, and re-layouts: 1.04 us -> 2.45 us
  transfers between devices with their start and end apart: 7 -> 7, of which waited for: 3 -> 5; matrix products, arithmetic and copies ran while one was open for 10% -> 0% of each run, Pallas kernels for 0% -> 5%
where the time goes in v2:
time: 129 us; the launch traced here: 128 us
  blocking collectives  40.9 us (32%)
  starting transfers between devices  37.5 us (29%)
  waiting for transfers between devices  36.1 us (28%)
  Pallas kernels  6.17 us (5%)
  local copies, waits for them, and re-layouts  4.08 us (3%)
  matrix products  2.91 us (2%)
    all_to_all x1, blocking collectives, on_device(): lax.all_to_all(result.reshape(experts_all, SLOTS, width), 'expert', 0, 0,...  40.9 us
    all_to_all x1, waiting for transfers between devices, on_device(): lax.all_to_all(slot_input.reshape(experts_all, SLOTS, width), 'expert', 0...  30.5 us
    all_to_all x1, starting transfers between devices, on_device(): lax.all_to_all(slot_input.reshape(experts_all, SLOTS, width), 'expert', 0...  21.6 us
    ppermute x2, starting transfers between devices, on_device(): others.append(lax.ppermute(piece, 'half', OTHER_CHIP))  5.84 us
    ppermute x2, starting transfers between devices, on_device(): returned = [lax.ppermute(term, 'half', OTHER_CHIP) for term in terms]  5.7 us
    pallas_call x3, Pallas kernels, experts_half(): pl.pallas_call(mlp_kernel, out_shape=jax.ShapeDtypeStruct((count, width),...  4.11 us
    ppermute x2, waiting for transfers between devices, on_device(): returned = [lax.ppermute(term, 'half', OTHER_CHIP) for term in terms]  3.91 us
  transfers between devices with their start and end apart: 7, of which 5 were waited for; matrix products, arithmetic and copies ran while one was open for 0% of the time, Pallas kernels for 5%

profile of v2, /device:TPU:32, one launch (start us, length us, event | category | flops | bytes accessed | tf_op | source)
XLA Modules:
  0.0 128.2 jit_solution(4024359485783416726)
XLA Ops:
  0.0 1.0 copy-done
  1.0 1.4 %fusion.6 = (f32[256]{0:T(256)S(1)}, f32[256]{0:T(256)S(1)}, f32[256,256]{1,0:T(8,128)S(1)}) fusion(bf16[256,1024]{1,0:T(8,128)(2,1)S(1)} %copy-done, bf16[1024,256]{1,0:T(8,128)(2,1)} %param.5), kind=kOutput, calls=%fused_computation.13 | convolution fusion | flops 134348288 | bytes 1312768 | tf_op jit(solution)/shard_map/md,dc->mc/dot_general | solution.py:81
  2.5 0.2 fusion
  2.7 0.0 copy-start.1
  2.7 0.3 convolution_convert_fusion.1
  3.0 1.0 reshape.16
  4.0 21.6 %all-to-all-start = ((bf16[128,2,1024]{2,1,0:T(2,128)(2,1)}), bf16[128,2,1024]{2,1,0:T(2,128)(2,1)S(1)}, u32[]{:S(2)}, u32[]{:S(2)}) async-start(bf16[128,2,1024]{2,1,0:T(2,128)(2,1)} %reshape.16), calls=%async_computation | async-start | bytes 1048576 | tf_op jit(solution)/shard_map/all_to_all | solution.py:87
  25.7 1.9 %collective-permute-start.1 = (bf16[1024,768]{1,0:T(8,128)(2,1)S(1)}, bf16[1024,768]{1,0:T(8,128)(2,1)}, u32[]{:S(2)}, u32[]{:S(2)}) collective-permute-start(bf16[1024,768]{1,0:T(8,128)(2,1)S(1)} %bitcast.6), channel_id=1, source_target_pairs={{0,1},{1,0},{2,3},{3,2},{4,5},{5,4},{6,7},{7,6},{8,9},{9,8},{10,11... | collective-permute-start | bytes 4718600 | tf_op jit(solution)/shard_map/ppermute | solution.py:91
  27.6 2.4 %collective-permute-start.2 = (bf16[768,1024]{1,0:T(8,128)(2,1)}, bf16[768,1024]{1,0:T(8,128)(2,1)}, u32[]{:S(2)}, u32[]{:S(2)}) collective-permute-start(bf16[768,1024]{1,0:T(8,128)(2,1)} %bitcast.8), channel_id=1, source_target_pairs={{0,1},{1,0},{2,3},{3,2},{4,5},{5,4},{6,7},{7,6},{8,9},{9,8},{10,11... | collective-permute-start | bytes 4718600 | tf_op jit(solution)/shard_map/ppermute | solution.py:92
  30.0 30.5 %all-to-all-done = bf16[128,2,1024]{2,1,0:T(2,128)(2,1)S(1)} async-done(((bf16[128,2,1024]{2,1,0:T(2,128)(2,1)}), bf16[128,2,1024]{2,1,0:T(2,128)(2,1)S(1)}, u32[]{:S(2)}, u32[]{:S(2)}) %all-to-all-start) | async-done | bytes 524320 | tf_op jit(solution)/shard_map/all_to_all | solution.py:87
  60.5 0.2 reshape.17.rows_ref
  60.8 2.6 %collective-permute-start = (bf16[128,1024]{1,0:T(8,128)(2,1)S(1)}, bf16[128,1024]{1,0:T(8,128)(2,1)S(1)}, u32[]{:S(2)}, u32[]{:S(2)}) collective-permute-start(bf16[128,1024]{1,0:T(8,128)(2,1)S(1)} %get-tuple-element.18), channel_id=1, source_target_pairs={{0,2},{1,3},{2,0},{3,1},{4,6},{5,7},{6,4},{7,5},{8,10},{9,11},{10,... | collective-permute-start | bytes 786440 | tf_op jit(solution)/shard_map/ppermute | solution.py:96
  63.3 3.3 %collective-permute-start.4 = (bf16[128,1024]{1,0:T(8,128)(2,1)S(1)}, bf16[128,1024]{1,0:T(8,128)(2,1)S(1)}, u32[]{:S(2)}, u32[]{:S(2)}) collective-permute-start(bf16[128,1024]{1,0:T(8,128)(2,1)S(1)} %get-tuple-element.17), channel_id=1, source_target_pairs={{0,2},{1,3},{2,0},{3,1},{4,6},{5,7},{6,4},{7,5},{8,10},{9,11},{10,... | collective-permute-start | bytes 786440 | tf_op jit(solution)/shard_map/ppermute | solution.py:96
  66.6 0.0 collective-permute-done.1.in_b
  66.6 0.0 collective-permute-done.2.out_b
  66.6 0.0 copy-start.2
  66.6 1.4 %copy-done.2 = bf16[1,768,1024]{2,1,0:T(8,128)(2,1)S(1)} copy-done((bf16[1,768,1024]{2,1,0:T(8,128)(2,1)S(1)}, bf16[1,768,1024]{2,1,0:T(8,128)(2,1)}, u32[]{:S(2)}) %copy-start.2) | copy-done | bytes 1572888
  68.0 2.1 %shard_map.46 = (bf16[1024,1536]{1,0:T(8,128)(2,1)S(1)}, bf16[1536,1024]{1,0:T(8,128)(2,1)S(1)}) custom-call(bf16[1024,768]{1,0:T(8,128)(2,1)S(1)} %bitcast.7, bf16[1024,768]{1,0:T(8,128)(2,1)} %collective-permute-done.1.in_b, bf16[768,1024]{1,0:T(8,128)(2,1)S(1)} %bitcast.9, bf16[768,1024]{1,0:T(8,128)(2,1)} %collective-permute-done.2.out_b), custom_call_target="tpu_custom_call" | custom-call | bytes 12582912 | tf_op jit(solution)/shard_map/pallas_call | solution.py:47
  70.1 1.4 %collective-permute-done.rows_ref = bf16[128,1024]{1,0:T(8,128)(2,1)S(1)} collective-permute-done((bf16[128,1024]{1,0:T(8,128)(2,1)S(1)}, bf16[128,1024]{1,0:T(8,128)(2,1)S(1)}, u32[]{:S(2)}, u32[]{:S(2)}) %collective-permute-start) | collective-permute-done | bytes 262176 | tf_op jit(solution)/shard_map/ppermute | solution.py:96
  71.6 1.1 shard_map.47
  72.6 2.8 %collective-permute-start.3 = (bf16[128,1024]{1,0:T(8,128)(2,1)S(1)}, bf16[128,1024]{1,0:T(8,128)(2,1)S(1)}, u32[]{:S(2)}, u32[]{:S(2)}) collective-permute-start(bf16[128,1024]{1,0:T(8,128)(2,1)S(1)} %shard_map.47), channel_id=1, source_target_pairs={{0,2},{1,3},{2,0},{3,1},{4,6},{5,7},{6,4},{7,5},{8,10},{9,11},{10,... | collective-permute-start | bytes 786440 | tf_op jit(solution)/shard_map/ppermute | solution.py:100
  75.4 0.3 collective-permute-done.4.rows_ref
  75.7 1.1 shard_map.49
  76.8 2.9 %collective-permute-start.5 = (bf16[128,1024]{1,0:T(8,128)(2,1)S(1)}, bf16[128,1024]{1,0:T(8,128)(2,1)S(1)}, u32[]{:S(2)}, u32[]{:S(2)}) collective-permute-start(bf16[128,1024]{1,0:T(8,128)(2,1)S(1)} %shard_map.49), channel_id=1, source_target_pairs={{0,2},{1,3},{2,0},{3,1},{4,6},{5,7},{6,4},{7,5},{8,10},{9,11},{10,... | collective-permute-start | bytes 786440 | tf_op jit(solution)/shard_map/ppermute | solution.py:100
  79.7 2.0 %shard_map.48 = f32[256,1024]{1,0:T(8,128)S(1)} custom-call(bf16[256,1024]{1,0:T(8,128)(2,1)S(1)} %reshape.17.rows_ref, bf16[1024,1536]{1,0:T(8,128)(2,1)S(1)} %get-tuple-element.9.in_ref, bf16[1536,1024]{1,0:T(8,128)(2,1)S(1)} %get-tuple-element.10.out_ref), custom_call_target="tpu_custom_call" | custom-call | flops 1610612736 | bytes 6291456 | tf_op jit(solution)/shard_map/pallas_call | solution.py:64
  81.7 1.1 collective-permute-done.3
  82.8 2.8 %collective-permute-done.5 = bf16[128,1024]{1,0:T(8,128)(2,1)S(1)} collective-permute-done((bf16[128,1024]{1,0:T(8,128)(2,1)S(1)}, bf16[128,1024]{1,0:T(8,128)(2,1)S(1)}, u32[]{:S(2)}, u32[]{:S(2)}) %collective-permute-start.5) | collective-permute-done | bytes 262176 | tf_op jit(solution)/shard_map/ppermute | solution.py:100
  85.6 0.1 add_convert_fusion
  85.7 0.2 reshape.18
  86.0 40.9 %all_to_all.10 = bf16[128,2,1024]{2,1,0:T(2,128)(2,1)S(1)} all-to-all(bf16[128,2,1024]{2,1,0:T(2,128)(2,1)S(1)} %reshape.18), channel_id=1, replica_groups=mesh['expert'=128,'half'=4] {'expert'}, dimensions={0} | all-to-all | bytes 1048576 | tf_op jit(solution)/shard_map/all_to_all | solution.py:102
  126.9 0.2 reshape.19
  127.1 1.2 convolution_convert_fusion
  (3 shorter events, 0.0 us)
Async XLA Ops:
  0.0 1.0 copy-start
  2.7 23.0 %copy-start.1 = (bf16[1,1024,768]{2,1,0:T(8,128)(2,1)S(1)}, bf16[1,1024,768]{2,1,0:T(8,128)(2,1)}, u32[]{:S(2)}) copy-start(bf16[1,1024,768]{2,1,0:T(8,128)(2,1)} %param.6) | copy-start | bytes 4718596
  4.0 56.5 %all-to-all-start = ((bf16[128,2,1024]{2,1,0:T(2,128)(2,1)}), bf16[128,2,1024]{2,1,0:T(2,128)(2,1)S(1)}, u32[]{:S(2)}, u32[]{:S(2)}) async-start(bf16[128,2,1024]{2,1,0:T(2,128)(2,1)} %reshape.16), calls=%async_computation | async-start | bytes 1048576 | tf_op jit(solution)/shard_map/all_to_all | solution.py:87
  25.7 41.0 %collective-permute-start.1 = (bf16[1024,768]{1,0:T(8,128)(2,1)S(1)}, bf16[1024,768]{1,0:T(8,128)(2,1)}, u32[]{:S(2)}, u32[]{:S(2)}) collective-permute-start(bf16[1024,768]{1,0:T(8,128)(2,1)S(1)} %bitcast.6), channel_id=1, source_target_pairs={{0,1},{1,0},{2,3},{3,2},{4,5},{5,4},{6,7},{7,6},{8,9},{9,8},{10,11... | collective-permute-start | bytes 4718600 | tf_op jit(solution)/shard_map/ppermute | solution.py:91
  27.6 39.0 %collective-permute-start.2 = (bf16[768,1024]{1,0:T(8,128)(2,1)}, bf16[768,1024]{1,0:T(8,128)(2,1)}, u32[]{:S(2)}, u32[]{:S(2)}) collective-permute-start(bf16[768,1024]{1,0:T(8,128)(2,1)} %bitcast.8), channel_id=1, source_target_pairs={{0,1},{1,0},{2,3},{3,2},{4,5},{5,4},{6,7},{7,6},{8,9},{9,8},{10,11... | collective-permute-start | bytes 4718600 | tf_op jit(solution)/shard_map/ppermute | solution.py:92
  60.8 10.8 %collective-permute-start = (bf16[128,1024]{1,0:T(8,128)(2,1)S(1)}, bf16[128,1024]{1,0:T(8,128)(2,1)S(1)}, u32[]{:S(2)}, u32[]{:S(2)}) collective-permute-start(bf16[128,1024]{1,0:T(8,128)(2,1)S(1)} %get-tuple-element.18), channel_id=1, source_target_pairs={{0,2},{1,3},{2,0},{3,1},{4,6},{5,7},{6,4},{7,5},{8,10},{9,11},{10,... | collective-permute-start | bytes 786440 | tf_op jit(solution)/shard_map/ppermute | solution.py:96
  63.3 12.3 %collective-permute-start.4 = (bf16[128,1024]{1,0:T(8,128)(2,1)S(1)}, bf16[128,1024]{1,0:T(8,128)(2,1)S(1)}, u32[]{:S(2)}, u32[]{:S(2)}) collective-permute-start(bf16[128,1024]{1,0:T(8,128)(2,1)S(1)} %get-tuple-element.17), channel_id=1, source_target_pairs={{0,2},{1,3},{2,0},{3,1},{4,6},{5,7},{6,4},{7,5},{8,10},{9,11},{10,... | collective-permute-start | bytes 786440 | tf_op jit(solution)/shard_map/ppermute | solution.py:96
  66.6 1.4 %copy-start.2 = (bf16[1,768,1024]{2,1,0:T(8,128)(2,1)S(1)}, bf16[1,768,1024]{2,1,0:T(8,128)(2,1)}, u32[]{:S(2)}) copy-start(bf16[1,768,1024]{2,1,0:T(8,128)(2,1)} %param.7) | copy-start | bytes 4718596
  72.6 10.2 %collective-permute-start.3 = (bf16[128,1024]{1,0:T(8,128)(2,1)S(1)}, bf16[128,1024]{1,0:T(8,128)(2,1)S(1)}, u32[]{:S(2)}, u32[]{:S(2)}) collective-permute-start(bf16[128,1024]{1,0:T(8,128)(2,1)S(1)} %shard_map.47), channel_id=1, source_target_pairs={{0,2},{1,3},{2,0},{3,1},{4,6},{5,7},{6,4},{7,5},{8,10},{9,11},{10,... | collective-permute-start | bytes 786440 | tf_op jit(solution)/shard_map/ppermute | solution.py:100
  76.8 8.8 %collective-permute-start.5 = (bf16[128,1024]{1,0:T(8,128)(2,1)S(1)}, bf16[128,1024]{1,0:T(8,128)(2,1)S(1)}, u32[]{:S(2)}, u32[]{:S(2)}) collective-permute-start(bf16[128,1024]{1,0:T(8,128)(2,1)S(1)} %shard_map.49), channel_id=1, source_target_pairs={{0,2},{1,3},{2,0},{3,1},{4,6},{5,7},{6,4},{7,5},{8,10},{9,11},{10,... | collective-permute-start | bytes 786440 | tf_op jit(solution)/shard_map/ppermute | solution.py:100
